TPU v7x, 32 devices: a whole 2x2x4 slice. The times are simulated.
32 devices in a mesh: depth: 2 (over x), wide: 16 (over z, y, core).
Axes of the slice: x: 2, y: 2, z: 4, core: 2. Of those that a mesh axis runs over, the one named last changes fastest.
Arguments:
- volume: bfloat16 [256, 128, 1024], P(('depth', 'wide')), may hold values from -6 to 6
- directions: int32 [2, 128], replicated, may hold values from 0 to 1
- light_dir: float32 [2, 3], replicated, may hold values from -4 to 4
- tf_center: float32 [2, 4], replicated, may hold values from -1.5 to 1.5
- tf_width: float32 [2, 4], replicated, may hold values from 0.2 to 0.8
- tf_height: float32 [2, 4], replicated, may hold values from 0.25 to 4
- tf_emission: float32 [2, 4, 3], replicated, may hold values from 0.5 to 6
Outputs:
- image_rgba: float32 [2, 4, 131072], P(None, None, ('depth', 'wide'))
Inputs may be any that keep to these rules, and one draw needn't show every extreme that they name: `directions`: 0 marks rays that run toward increasing depth index, 1 rays that run toward decreasing depth index.
All inputs are finite; a program needn't handle non-finite values.
Results may differ from a plain program's by a relative error of at most 0.0003.
Values may be sent and summed in bfloat16 or wider, within the bound.
A program may use at most 64 MiB of HBM per device.

v0:
```python
import functools
import math

import jax
import jax.numpy as jnp
from jax import lax
from jax.experimental import pallas as pl
from jax.experimental.pallas import tpu as pltpu
from jax.sharding import PartitionSpec as P

AMBIENT = 0.3
DIFFUSE = 0.7


def padded_2(block, sides, width):
    for axis, dim in sides:
        count = lax.axis_size(axis)
        forward = [(i, i + 1) for i in range(count - 1)]
        backward = [(target, source) for source, target in forward]
        low = lax.ppermute(
            lax.slice_in_dim(block, block.shape[dim] - width, None, axis=dim), axis, forward
        )
        high = lax.ppermute(lax.slice_in_dim(block, 0, width, axis=dim), axis, backward)
        block = jnp.concatenate([low, block, high], axis=dim)
    return block


def partner(block, axis, distance):
    count = lax.axis_size(axis)
    route = []
    for low in range(count):
        high = low | 1 << distance
        if high != low and high < count:
            route += [(low, high), (high, low)]
    return lax.ppermute(block, axis, route)


def shifted_diff(values, along_axis):
    padding = [(0, 0)] * values.ndim
    padding[along_axis] = (1, 1)
    padded = jnp.pad(values, padding)
    length_now = values.shape[along_axis]
    upper_part = lax.slice_in_dim(padded, 2, length_now + 2, 1, along_axis)
    lower_part = lax.slice_in_dim(padded, 0, length_now, 1, along_axis)
    return 0.5 * (upper_part - lower_part)


def layer_rgba(
    layer_below,
    center_layer,
    layer_above,
    light_dir,
    tf_center,
    tf_width,
    tf_height,
    tf_emission,
    depth_step,
):
    grad_z = 0.5 * (layer_above - layer_below)
    grad_y = shifted_diff(center_layer, 0)
    grad_x = shifted_diff(center_layer, 1)
    lighting = jnp.abs(
        grad_z[None] * light_dir[:, 0, None, None]
        + grad_y[None] * light_dir[:, 1, None, None]
        + grad_x[None] * light_dir[:, 2, None, None]
    )
    magnitude = jnp.sqrt(grad_x * grad_x + grad_y * grad_y + grad_z * grad_z + 1.0)
    shading = AMBIENT + DIFFUSE * lighting / magnitude[None]
    scaled = (center_layer[None, None] - tf_center[:, :, None, None]) / tf_width[:, :, None, None]
    bumps = jnp.exp(-scaled * scaled)
    density = jnp.sum(tf_height[:, :, None, None] * bumps, axis=1)
    weights = tf_height[:, :, None] * tf_emission
    tinted = jnp.einsum("vkc,vkhw->vchw", weights, bumps, precision=lax.Precision.HIGHEST)
    colour = depth_step * shading[:, None] * tinted
    opacity = 1.0 - jnp.exp(-depth_step * density)
    sample_rgba = jnp.concatenate([colour, opacity[:, None]], axis=1)
    return sample_rgba.reshape(sample_rgba.shape[0], 4, -1)


def over_ordered(lower_part, upper_part, flags):
    front_first = lower_part + (1.0 - lower_part[:, 3:4]) * upper_part
    back_first = upper_part + (1.0 - upper_part[:, 3:4]) * lower_part
    return jnp.where(flags, back_first, front_first)


def split_pair(values, along_axis):
    array_shape = values.shape
    new_shape = (
        array_shape[:along_axis] + (array_shape[along_axis] // 2, 2) + array_shape[along_axis + 1 :]
    )
    paired = values.reshape(new_shape)
    first_half = lax.index_in_dim(paired, 0, along_axis + 1, keepdims=False)
    second_half = lax.index_in_dim(paired, 1, along_axis + 1, keepdims=False)
    return (first_half, second_half)


def plain_body(volume, directions, light_dir, tf_center, tf_width, tf_height, tf_emission):
    depth_count = lax.axis_size("depth")
    wide_count = lax.axis_size("wide")
    slab_cells = volume.shape[0]
    depth_step = 1.0 / (slab_cells * depth_count * wide_count)
    view_count = light_dir.shape[0]
    pixel_count = volume.shape[1] * volume.shape[2]
    flags = jnp.repeat(directions == 1, volume.shape[2], axis=1)[:, None, :]
    padded = padded_2(volume, ((("depth", "wide"), 0),), 1)

    def advance(layer_index, composite):
        layers = lax.dynamic_slice_in_dim(padded, layer_index, 3, 0).astype(jnp.float32)
        sample_rgba = layer_rgba(
            layers[0],
            layers[1],
            layers[2],
            light_dir,
            tf_center,
            tf_width,
            tf_height,
            tf_emission,
            depth_step,
        )
        return over_ordered(composite, sample_rgba, flags)

    initial = jnp.zeros((view_count, 4, pixel_count), jnp.float32)
    slab_image = lax.fori_loop(0, slab_cells, advance, initial)
    block_pixels = pixel_count // (depth_count * wide_count)
    blocked = slab_image.reshape(view_count, 4, depth_count, wide_count, block_pixels)
    blocked_flags = flags.reshape(view_count, 1, depth_count, wide_count, block_pixels)
    wide_index = lax.axis_index("wide")
    depth_index = lax.axis_index("depth")
    merged = blocked
    merged_flags = blocked_flags
    for bit_number in range(wide_count.bit_length() - 1):
        own_bit = wide_index >> bit_number & 1
        first_half, second_half = split_pair(merged, 3)
        flag_first, flag_second = split_pair(merged_flags, 3)
        kept = jnp.where(own_bit == 0, first_half, second_half)
        outgoing = jnp.where(own_bit == 0, second_half, first_half)
        merged_flags = jnp.where(own_bit == 0, flag_first, flag_second)
        incoming = partner(outgoing, "wide", bit_number)
        merged = jnp.where(
            own_bit == 0,
            over_ordered(kept, incoming, merged_flags),
            over_ordered(incoming, kept, merged_flags),
        )
    range_image = jnp.squeeze(merged, 3)
    range_flags = jnp.squeeze(merged_flags, 3)
    merged = range_image
    merged_flags = range_flags
    for bit_number in range(depth_count.bit_length() - 1):
        own_bit = depth_index >> bit_number & 1
        first_half, second_half = split_pair(merged, 2)
        flag_first, flag_second = split_pair(merged_flags, 2)
        kept = jnp.where(own_bit == 0, first_half, second_half)
        outgoing = jnp.where(own_bit == 0, second_half, first_half)
        merged_flags = jnp.where(own_bit == 0, flag_first, flag_second)
        incoming = partner(outgoing, "depth", bit_number)
        merged = jnp.where(
            own_bit == 0,
            over_ordered(kept, incoming, merged_flags),
            over_ordered(incoming, kept, merged_flags),
        )
    final_block = jnp.squeeze(merged, 2)
    return final_block


MESH = pl.DeviceIdType.MESH
LOG2E = math.log2(math.e)
LANES = 256
ROWS = 16
LAG_CORE, LAG_Y, LAG_Z0, LAG_Z1, LAG_X = 2, 5, 8, 12, 15


def kernel(
    layer_total, chunks, groups,
    vol, dirs, light, center, width, height, tint,
    out,
    xf, halo, flagv, cst, obuf, cbuf, ysend, ybuf, zbuf, wbuf, xbuf, fin,
    halo_ss, halo_rs, send_sem, recv_sem, fin_ss, fin_rs,
):
    slab, rows, cols = vol.shape
    step = 1.0 / layer_total
    x = lax.axis_index("depth")
    w = lax.axis_index("wide")
    c = lax.rem(w, 2)
    y = lax.rem(lax.div(w, 2), 2)
    z0 = lax.rem(lax.div(w, 4), 2)
    z1 = lax.div(w, 8)
    me = x * 16 + w
    peers = (
        (x, w + 1 - 2 * c),
        (x, w + 2 - 4 * y),
        (x, w + 4 - 8 * z0),
        (x, w + 8 - 16 * z1),
        (1 - x, w),
    )
    core_peer, y_peer, z0_peer, z1_peer, x_peer = peers
    after = lax.rem(me + 1, 32)
    before = lax.rem(me + 31, 32)
    next_dev = (lax.div(after, 16), lax.rem(after, 16))
    prev_dev = (lax.div(before, 16), lax.rem(before, 16))
    has_prev = me > 0
    has_next = me < 31

    barrier = pltpu.get_barrier_semaphore()
    for peer in peers + (next_dev, prev_dev):
        pl.semaphore_signal(barrier, inc=1, device_id=peer, device_id_type=MESH)
    pl.semaphore_wait(barrier, 7)

    quarters = cols // LANES

    def up_copy(q):
        return pltpu.make_async_remote_copy(
            src_ref=vol.at[slab - 1, :, pl.ds(pl.multiple_of(q * LANES, LANES), LANES)],
            dst_ref=halo.at[0, q], send_sem=halo_ss.at[0, q], recv_sem=halo_rs.at[0, q],
            device_id=next_dev, device_id_type=MESH)

    def down_copy(q):
        return pltpu.make_async_remote_copy(
            src_ref=vol.at[0, :, pl.ds(pl.multiple_of(q * LANES, LANES), LANES)],
            dst_ref=halo.at[1, q], send_sem=halo_ss.at[1, q], recv_sem=halo_rs.at[1, q],
            device_id=prev_dev, device_id_type=MESH)

    for q in range(quarters):
        @pl.when(has_next)
        def _():
            up_copy(q).start()

        @pl.when(has_prev)
        def _():
            down_copy(q).start()

    for v in range(2):
        for k in range(4):
            full = lambda ref: jnp.full((8, 128), ref[v, k], jnp.float32)
            scale = math.sqrt(LOG2E) / full(width)
            cst[v * 15 + k] = scale
            cst[v * 15 + 4 + k] = scale * full(center)
            cst[v * 15 + 8 + k] = jnp.log(full(height) * (step * LOG2E)) * LOG2E
        for a in range(3):
            cst[v * 15 + 12 + a] = jnp.full((8, 128), DIFFUSE * light[v, a], jnp.float32)
    row_of = lax.broadcasted_iota(jnp.int32, (8, 128), 0)
    lane_of = lax.broadcasted_iota(jnp.int32, (8, 128), 1)

    def fill_flags(g, carry):
        for v in range(2):
            value = jnp.zeros((8, 128), jnp.float32)
            for i in range(8):
                value = jnp.where(row_of == i, dirs[v, g * 8 + i].astype(jnp.float32), value)
            flagv[v, g] = value
        return carry

    lax.fori_loop(0, rows // 8, fill_flags, 0)

    def pad(z, carry):
        xf[z, 0:8, :] = jnp.zeros((8, cols + 256), jnp.float32)
        xf[z, rows + 8:rows + 16, :] = jnp.zeros((8, cols + 256), jnp.float32)
        xf[z, 8:rows + 8, 0:128] = jnp.zeros((rows, 128), jnp.float32)
        xf[z, 8:rows + 8, cols + 128:cols + 256] = jnp.zeros((rows, 128), jnp.float32)

        def widen(b, inner):
            xf[z, pl.ds(pl.multiple_of(b * 16 + 8, 8), 16), 128:cols + 128] = vol[
                z - 1, pl.ds(pl.multiple_of(b * 16, 16), 16), :
            ].astype(jnp.float32)
            return inner

        return lax.fori_loop(0, rows // 16, widen, carry)

    lax.fori_loop(1, slab + 1, pad, 0)

    def take_halo(side, place, present, copy, q):
        lanes = pl.ds(pl.multiple_of(q * LANES + 128, 128), LANES)

        @pl.when(present)
        def _():
            copy(q).wait_recv()
            xf[place, 8:rows + 8, lanes] = halo[side, q].astype(jnp.float32)

        @pl.when(jnp.logical_not(present))
        def _():
            xf[place, 8:rows + 8, lanes] = jnp.zeros((rows, LANES), jnp.float32)

    def place_of(k):
        return lax.rem(k, groups), lax.div(k, groups)

    def render(k):
        j, q = place_of(k)

        def tile(t, carry):
            h = lax.div(t, 2)
            p = lax.rem(t, 2)
            g = j * 2 + h
            r0 = pl.multiple_of(g * 8 + 8, 8)
            l0 = pl.multiple_of(q * LANES + p * 128 + 128, 128)
            here_rows, here_lanes = pl.ds(r0, 8), pl.ds(l0, 128)
            flags = [flagv[v, g] > 0.5 for v in range(2)]
            signs = [jnp.where(f, 1.0, -1.0) for f in flags]
            run = [jnp.zeros((8, 128), jnp.float32)] * 2
            sums = [[jnp.zeros((8, 128), jnp.float32)] * 4 for v in range(2)]
            for z in range(1, slab + 1):
                here = xf[z, here_rows, here_lanes]
                left = xf[z, here_rows, pl.ds(pl.multiple_of(l0 - 128, 128), 128)]
                right = xf[z, here_rows, pl.ds(pl.multiple_of(l0 + 128, 128), 128)]
                above = xf[z, pl.ds(pl.multiple_of(r0 - 8, 8), 8), here_lanes]
                below = xf[z, pl.ds(pl.multiple_of(r0 + 8, 8), 8), here_lanes]
                gz = xf[z + 1, here_rows, here_lanes] - xf[z - 1, here_rows, here_lanes]
                gx = pltpu.roll(jnp.where(lane_of == 0, right, here), 127, 1) - pltpu.roll(
                    jnp.where(lane_of == 127, left, here), 1, 1)
                gy = pltpu.roll(jnp.where(row_of == 0, below, here), 7, 0) - pltpu.roll(
                    jnp.where(row_of == 7, above, here), 1, 0)
                inverse = lax.rsqrt(gx * gx + gy * gy + (gz * gz + 4.0))
                for v in range(2):
                    dot = gz * cst[v * 15 + 12] + gy * cst[v * 15 + 13] + gx * cst[v * 15 + 14]
                    shade = jnp.abs(dot) * inverse + AMBIENT
                    bumps = []
                    for b in range(4):
                        u = here * cst[v * 15 + b] - cst[v * 15 + 4 + b]
                        bumps.append(jnp.exp2(cst[v * 15 + 8 + b] - u * u))
                    thick = (bumps[0] + bumps[1]) + (bumps[2] + bumps[3])
                    later = run[v] + signs[v] * thick
                    weight = jnp.exp2(jnp.where(flags[v], later, run[v])) * shade
                    run[v] = later
                    sums[v] = [s + weight * b for s, b in zip(sums[v], bumps)]
            lanes = pl.ds(pl.multiple_of(p * 128, 128), 128)
            for v in range(2):
                clear = jnp.exp2(-signs[v] * run[v])
                front = jnp.where(flags[v], clear, 1.0)
                scaled = [s * front for s in sums[v]]
                parts = []
                for ch in range(3):
                    total = scaled[0] * (tint[v, 0, ch] * (1.0 / LOG2E))
                    for b in range(1, 4):
                        total = total + scaled[b] * (tint[v, b, ch] * (1.0 / LOG2E))
                    parts.append(total)
                parts.append(clear)

                @pl.when(c == v)
                def _():
                    for ch in range(4):
                        cbuf[c, k, h, ch, :, lanes] = parts[ch]

                @pl.when(c != v)
                def _():
                    for ch in range(4):
                        obuf[k, h, ch, :, lanes] = parts[ch]
            return carry

        lax.fori_loop(0, 4, tile, 0)

    def merged(low, high, flag):
        lt, ut = low(3), high(3)
        p = jnp.where(flag, ut, 1.0)
        o = jnp.where(flag, 1.0, lt)
        return [p * low(ch) + o * high(ch) for ch in range(3)] + [lt * ut]

    def merge(low, high, flag_tile, store):
        for p in range(LANES // 128):
            s = slice(p * 128, p * 128 + 128)
            parts = merged(lambda ch: low[ch, :, s], lambda ch: high[ch, :, s], flag_tile > 0.5)
            for ch in range(4):
                store[ch, :, s] = parts[ch]

    def core_copy(k):
        return pltpu.make_async_remote_copy(
            src_ref=obuf.at[k], dst_ref=cbuf.at[c, k], send_sem=send_sem.at[0, k],
            recv_sem=recv_sem.at[0, k], device_id=core_peer, device_id_type=MESH)

    def y_copy(k):
        return pltpu.make_async_remote_copy(
            src_ref=ysend.at[k], dst_ref=ybuf.at[y, k], send_sem=send_sem.at[1, k],
            recv_sem=recv_sem.at[1, k], device_id=y_peer, device_id_type=MESH)

    def pass_on(buf, bit, stage, peer):
        return lambda k: pltpu.make_async_remote_copy(
            src_ref=buf.at[bit, k], dst_ref=buf.at[bit, k], send_sem=send_sem.at[stage, k],
            recv_sem=recv_sem.at[stage, k], device_id=peer, device_id_type=MESH)

    z0_copy = pass_on(zbuf, z0, 2, z0_peer)
    z1_copy = pass_on(wbuf, z1, 3, z1_peer)
    x_copy = pass_on(xbuf, x, 4, x_peer)

    def bits(k):
        j = lax.rem(k, groups)
        return lax.rem(j, 2), lax.rem(lax.div(j, 2), 2), lax.div(j, 4)

    def held(k):
        b0, b1, bx = bits(k)
        at0 = b0 == z0
        at1 = jnp.logical_and(at0, b1 == z1)
        return at0, at1, jnp.logical_and(at1, bx == x)

    def group_flag(k, half):
        return flagv[c, lax.rem(k, groups) * 2 + half]

    def inside(i, lag):
        return jnp.logical_and(i >= lag, i < chunks + lag)

    def advance(i, carry):
        @pl.when(jnp.logical_and(i < chunks, lax.rem(i, groups) == 0))
        def _():
            q = lax.div(i, groups)
            take_halo(0, 0, has_prev, up_copy, q)
            take_halo(1, slab + 1, has_next, down_copy, q)

        @pl.when(i < chunks)
        def _():
            render(i)
            core_copy(i).start()

        @pl.when(inside(i, LAG_CORE))
        def _():
            k = i - LAG_CORE
            core_copy(k).wait_recv()
            merge(cbuf.at[0, k, 1 - y], cbuf.at[1, k, 1 - y], group_flag(k, 1 - y), ysend.at[k])
            y_copy(k).start()
            merge(cbuf.at[0, k, y], cbuf.at[1, k, y], group_flag(k, y), ybuf.at[y, k])

        @pl.when(inside(i, LAG_Y))
        def _():
            k = i - LAG_Y
            y_copy(k).wait_recv()
            merge(ybuf.at[0, k], ybuf.at[1, k], group_flag(k, y), zbuf.at[z0, k])

            @pl.when(jnp.logical_not(held(k)[0]))
            def _():
                z0_copy(k).start()

        @pl.when(jnp.logical_and(inside(i, LAG_Z0), held(i + groups * 4 - LAG_Z0)[0]))
        def _():
            k = i - LAG_Z0
            z0_copy(k).wait_recv()
            merge(zbuf.at[0, k], zbuf.at[1, k], group_flag(k, y), wbuf.at[z1, k])

            @pl.when(jnp.logical_not(held(k)[1]))
            def _():
                z1_copy(k).start()

        @pl.when(jnp.logical_and(inside(i, LAG_Z1), held(i + groups * 4 - LAG_Z1)[1]))
        def _():
            k = i - LAG_Z1
            z1_copy(k).wait_recv()
            merge(wbuf.at[0, k], wbuf.at[1, k], group_flag(k, y), xbuf.at[x, k])

            @pl.when(jnp.logical_not(held(k)[2]))
            def _():
                x_copy(k).start()

        @pl.when(jnp.logical_and(inside(i, LAG_X), held(i + groups * 4 - LAG_X)[2]))
        def _():
            k = i - LAG_X
            x_copy(k).wait_recv()
            flag = group_flag(k, y) > 0.5
            for p in range(LANES // 128):
                s = slice(p * 128, p * 128 + 128)
                parts = merged(lambda ch: xbuf[0, k, ch, :, s], lambda ch: xbuf[1, k, ch, :, s], flag)
                parts[3] = 1.0 - parts[3]
                for r in range(8):
                    start = (r % 4) * cols + lax.div(k, groups) * LANES + p * 128
                    spot = pl.ds(pl.multiple_of(start, 128), 128)
                    for ch in range(4):
                        fin[r // 4, ch:ch + 1, spot] = parts[ch][r:r + 1, :]

        return carry

    lax.fori_loop(0, chunks + LAG_X, advance, 0)

    last = pltpu.make_async_remote_copy(
        src_ref=fin.at[1 - c], dst_ref=out.at[c], send_sem=fin_ss, recv_sem=fin_rs,
        device_id=core_peer, device_id_type=MESH)
    last.start()
    out[c] = fin[c]

    def settle(k, carry):
        core_copy(k).wait_send()
        y_copy(k).wait_send()
        at0, at1, at2 = held(k)

        @pl.when(jnp.logical_not(at0))
        def _():
            z0_copy(k).wait_send()

        @pl.when(jnp.logical_and(at0, jnp.logical_not(at1)))
        def _():
            z1_copy(k).wait_send()

        @pl.when(jnp.logical_and(at1, jnp.logical_not(at2)))
        def _():
            x_copy(k).wait_send()

        return carry

    lax.fori_loop(0, chunks, settle, 0)
    for q in range(quarters):
        @pl.when(has_next)
        def _():
            up_copy(q).wait_send()

        @pl.when(has_prev)
        def _():
            down_copy(q).wait_send()
    last.wait()


def fused_body(volume, directions, light_dir, tf_center, tf_width, tf_height, tf_emission):
    slab, rows, cols = volume.shape
    devices = lax.axis_size("depth") * lax.axis_size("wide")
    quarters = cols // LANES
    groups = rows // ROWS
    chunks = groups * quarters
    f32 = jnp.float32
    piece = (4, 8, LANES)
    vmem = pl.BlockSpec(memory_space=pltpu.VMEM)
    smem = pl.BlockSpec(memory_space=pltpu.SMEM)
    return pl.pallas_call(
        functools.partial(kernel, slab * devices, chunks, groups),
        out_shape=jax.ShapeDtypeStruct((2, 4, rows * cols // devices), f32),
        in_specs=[vmem] + [smem] * 6,
        out_specs=vmem,
        scratch_shapes=[
            pltpu.VMEM((slab + 2, rows + 16, cols + 256), f32),
            pltpu.VMEM((2, quarters, rows, LANES), volume.dtype),
            pltpu.VMEM((2, rows // 8, 8, 128), f32),
            pltpu.VMEM((30, 8, 128), f32),
            pltpu.VMEM((chunks, 2) + piece, f32),
            pltpu.VMEM((2, chunks, 2) + piece, f32),
            pltpu.VMEM((chunks,) + piece, f32),
            pltpu.VMEM((2, chunks) + piece, f32),
            pltpu.VMEM((2, chunks) + piece, f32),
            pltpu.VMEM((2, chunks) + piece, f32),
            pltpu.VMEM((2, chunks) + piece, f32),
            pltpu.VMEM((2, 4, rows * cols // devices), f32),
            pltpu.SemaphoreType.DMA((2, quarters)),
            pltpu.SemaphoreType.DMA((2, quarters)),
            pltpu.SemaphoreType.DMA((5, chunks)),
            pltpu.SemaphoreType.DMA((5, chunks)),
            pltpu.SemaphoreType.DMA,
            pltpu.SemaphoreType.DMA,
        ],
        compiler_params=pltpu.CompilerParams(
            collective_id=0, has_side_effects=True, vmem_limit_bytes=48 * 1024 * 1024
        ),
    )(volume, directions, light_dir, tf_center, tf_width, tf_height, tf_emission)


def body(volume, *parameters):
    slab, rows, cols = volume.shape
    fused = (
        lax.axis_size("depth") == 2
        and lax.axis_size("wide") == 16
        and rows == 128
        and cols % LANES == 0
    )
    return (fused_body if fused else plain_body)(volume, *parameters)


def solution(mesh):
    return jax.shard_map(
        body,
        mesh=mesh,
        in_specs=(P(("depth", "wide"), None, None), P(), P(), P(), P(), P(), P()),
        out_specs=P(None, None, ("depth", "wide")),
        check_vma=False,
    )
```

profile of v0, /device:TPU:27, one launch (start us, length us, event | category | flops | bytes accessed | tf_op | source)
XLA Modules:
  0.0 62.4 jit_solution(10407040583026241288)
XLA Ops:
  0.0 0.8 %copy.8.tint = f32[2,4,3]{2,1,0:T(4,128)S(1)} copy(f32[2,4,3]{1,0,2:T(2,128)} %param.13) | data formatting | bytes 192 | tf_op args[6]
  0.8 0.0 copy-start
  0.8 1.6 %copy-done = bf16[8,128,1024]{2,1,0:T(8,128)(2,1)S(1)} copy-done((bf16[8,128,1024]{2,1,0:T(8,128)(2,1)S(1)}, bf16[8,128,1024]{2,1,0:T(8,128)(2,1)}, u32[]{:S(2)}) %copy-start) | copy-done | bytes 2097176
  2.4 0.0 copy-start.1
  2.4 0.7 %copy-done.1 = s32[2,128]{1,0:T(2,128)S(1)} copy-done((s32[2,128]{1,0:T(2,128)S(1)}, s32[2,128]{1,0:T(2,128)}, u32[]{:S(2)}) %copy-start.1) | copy-done | bytes 1048
  3.0 0.0 copy-start.2
  3.0 0.7 %copy-done.2 = f32[2,3]{1,0:T(2,128)S(1)} copy-done((f32[2,3]{1,0:T(2,128)S(1)}, f32[2,3]{1,0:T(2,128)}, u32[]{:S(2)}) %copy-start.2) | copy-done | bytes 48
  3.7 0.0 copy-start.3
  3.7 0.7 %copy-done.3 = f32[2,4]{1,0:T(2,128)S(1)} copy-done((f32[2,4]{1,0:T(2,128)S(1)}, f32[2,4]{1,0:T(2,128)}, u32[]{:S(2)}) %copy-start.3) | copy-done | bytes 56
  4.4 0.0 copy-start.4
  4.4 0.7 %copy-done.4 = f32[2,4]{1,0:T(2,128)S(1)} copy-done((f32[2,4]{1,0:T(2,128)S(1)}, f32[2,4]{1,0:T(2,128)}, u32[]{:S(2)}) %copy-start.4) | copy-done | bytes 56
  5.1 0.0 copy-start.5
  5.1 0.7 %copy-done.5 = f32[2,4]{1,0:T(2,128)S(1)} copy-done((f32[2,4]{1,0:T(2,128)S(1)}, f32[2,4]{1,0:T(2,128)}, u32[]{:S(2)}) %copy-start.5) | copy-done | bytes 56
  5.8 55.9 %shard_map.73 = f32[2,4,4096]{2,1,0:T(4,128)S(1)} custom-call(bf16[8,128,1024]{2,1,0:T(8,128)(2,1)S(1)} %copy-done, s32[2,128]{1,0:T(2,128)S(1)} %copy-done.1, f32[2,3]{1,0:T(2,128)S(1)} %copy-done.2, f32[2,4]{1,0:T(2,128)S(1)} %copy-done.3, f32[2,4]{1,0:T(2,128)S(1)} %copy-done.4, f32[2,4]{1,0:T(2,128)S(1)} %copy-done.5, f32[2,4,3]{2,1,0:T(4,128)S(1)} %copy.8.tint), custom_call_target="tpu_custom_call" | custom-call | tf_op jit(solution)/shard_map/pallas_call | solution.py:512
  61.7 0.7 %copy.10 = f32[2,4,4096]{2,1,0:T(4,128)} copy(f32[2,4,4096]{2,1,0:T(4,128)S(1)} %shard_map.73) | data formatting | bytes 262144
Async XLA Ops:
  0.8 1.6 %copy-start = (bf16[8,128,1024]{2,1,0:T(8,128)(2,1)S(1)}, bf16[8,128,1024]{2,1,0:T(8,128)(2,1)}, u32[]{:S(2)}) copy-start(bf16[8,128,1024]{2,1,0:T(8,128)(2,1)} %vol.1) | copy-start | bytes 6291460
  2.4 0.7 %copy-start.1 = (s32[2,128]{1,0:T(2,128)S(1)}, s32[2,128]{1,0:T(2,128)}, u32[]{:S(2)}) copy-start(s32[2,128]{1,0:T(2,128)} %dirs.1) | copy-start | bytes 3076
  3.0 0.7 %copy-start.2 = (f32[2,3]{1,0:T(2,128)S(1)}, f32[2,3]{1,0:T(2,128)}, u32[]{:S(2)}) copy-start(f32[2,3]{1,0:T(2,128)} %light.1) | copy-start | bytes 76
  3.7 0.7 %copy-start.3 = (f32[2,4]{1,0:T(2,128)S(1)}, f32[2,4]{1,0:T(2,128)}, u32[]{:S(2)}) copy-start(f32[2,4]{1,0:T(2,128)} %center.1) | copy-start | bytes 100
  4.4 0.7 %copy-start.4 = (f32[2,4]{1,0:T(2,128)S(1)}, f32[2,4]{1,0:T(2,128)}, u32[]{:S(2)}) copy-start(f32[2,4]{1,0:T(2,128)} %width.1) | copy-start | bytes 100
  5.1 0.7 %copy-start.5 = (f32[2,4]{1,0:T(2,128)S(1)}, f32[2,4]{1,0:T(2,128)}, u32[]{:S(2)}) copy-start(f32[2,4]{1,0:T(2,128)} %height.1) | copy-start | bytes 100
where the time goes:
time: 62.6 us; the launch traced here: 62.4 us
  Pallas kernels  55.9 us (89%)
  local copies, waits for them, and re-layouts  6.42 us (10%)
    pallas_call x1, Pallas kernels, fused_body(): pl.pallas_call(functools.partial(kernel, slab * devices, chunks, groups),...  55.9 us
    unnamed x14, local copies, waits for them, and re-layouts  6.42 us

commit v1 on v0

--- a/solution.py
+++ b/solution.py
@@ -166,13 +166,14 @@
 LOG2E = math.log2(math.e)
 LANES = 256
 ROWS = 16
-LAG_CORE, LAG_Y, LAG_Z0, LAG_Z1, LAG_X = 2, 5, 8, 12, 15
+LAG_CORE, LAG_Y, LAG_Z0, LAG_Z1, LAG_X = 3, 8, 13, 18, 22
 
 
 def kernel(
     layer_total, chunks, groups,
-    vol, dirs, light, center, width, height, tint,
+    vol, dirs_in, light_in, center_in, width_in, height_in, tint_in,
     out,
+    slabs, dirs, light, center, width, height, tint, in_sems,
     xf, halo, flagv, cst, obuf, cbuf, ysend, ybuf, zbuf, wbuf, xbuf, fin,
     halo_ss, halo_rs, send_sem, recv_sem, fin_ss, fin_rs,
 ):
@@ -200,9 +201,22 @@
     has_prev = me > 0
     has_next = me < 31
 
+    given = (
+        (dirs_in, dirs), (light_in, light), (center_in, center), (width_in, width),
+        (height_in, height), (tint_in, tint),
+    )
+    small = [pltpu.make_async_copy(a, b, in_sems.at[n]) for n, (a, b) in enumerate(given)]
+
+    def slab_copy(z):
+        return pltpu.make_async_copy(vol.at[z], slabs.at[z], in_sems.at[6 + z])
+
     barrier = pltpu.get_barrier_semaphore()
     for peer in peers + (next_dev, prev_dev):
         pl.semaphore_signal(barrier, inc=1, device_id=peer, device_id_type=MESH)
+    for copy in small:
+        copy.start()
+    for z in range(slab):
+        slab_copy(z).start()
     pl.semaphore_wait(barrier, 7)
 
     quarters = cols // LANES
@@ -228,6 +242,8 @@
         def _():
             down_copy(q).start()
 
+    for copy in small:
+        copy.wait()
     for v in range(2):
         for k in range(4):
             full = lambda ref: jnp.full((8, 128), ref[v, k], jnp.float32)
@@ -251,13 +267,14 @@
     lax.fori_loop(0, rows // 8, fill_flags, 0)
 
     def pad(z, carry):
+        slab_copy(z - 1).wait()
         xf[z, 0:8, :] = jnp.zeros((8, cols + 256), jnp.float32)
         xf[z, rows + 8:rows + 16, :] = jnp.zeros((8, cols + 256), jnp.float32)
         xf[z, 8:rows + 8, 0:128] = jnp.zeros((rows, 128), jnp.float32)
         xf[z, 8:rows + 8, cols + 128:cols + 256] = jnp.zeros((rows, 128), jnp.float32)
 
         def widen(b, inner):
-            xf[z, pl.ds(pl.multiple_of(b * 16 + 8, 8), 16), 128:cols + 128] = vol[
+            xf[z, pl.ds(pl.multiple_of(b * 16 + 8, 8), 16), 128:cols + 128] = slabs[
                 z - 1, pl.ds(pl.multiple_of(b * 16, 16), 16), :
             ].astype(jnp.float32)
             return inner
@@ -326,9 +343,9 @@
                 scaled = [s * front for s in sums[v]]
                 parts = []
                 for ch in range(3):
-                    total = scaled[0] * (tint[v, 0, ch] * (1.0 / LOG2E))
+                    total = scaled[0] * (tint[ch, v, 0] * (1.0 / LOG2E))
                     for b in range(1, 4):
-                        total = total + scaled[b] * (tint[v, b, ch] * (1.0 / LOG2E))
+                        total = total + scaled[b] * (tint[ch, v, b] * (1.0 / LOG2E))
                     parts.append(total)
                 parts.append(clear)
 
@@ -508,13 +525,19 @@
     f32 = jnp.float32
     piece = (4, 8, LANES)
     vmem = pl.BlockSpec(memory_space=pltpu.VMEM)
-    smem = pl.BlockSpec(memory_space=pltpu.SMEM)
+    hbm = pl.BlockSpec(memory_space=pltpu.HBM)
+    parameters = (
+        directions, light_dir, tf_center, tf_width, tf_height, jnp.transpose(tf_emission, (2, 0, 1))
+    )
     return pl.pallas_call(
         functools.partial(kernel, slab * devices, chunks, groups),
         out_shape=jax.ShapeDtypeStruct((2, 4, rows * cols // devices), f32),
-        in_specs=[vmem] + [smem] * 6,
+        in_specs=[hbm] * 7,
         out_specs=vmem,
-        scratch_shapes=[
+        scratch_shapes=[pltpu.VMEM(volume.shape, volume.dtype)]
+        + [pltpu.SMEM(p.shape, p.dtype) for p in parameters]
+        + [
+            pltpu.SemaphoreType.DMA((6 + slab,)),
             pltpu.VMEM((slab + 2, rows + 16, cols + 256), f32),
             pltpu.VMEM((2, quarters, rows, LANES), volume.dtype),
             pltpu.VMEM((2, rows // 8, 8, 128), f32),
@@ -535,9 +558,9 @@
             pltpu.SemaphoreType.DMA,
         ],
         compiler_params=pltpu.CompilerParams(
-            collective_id=0, has_side_effects=True, vmem_limit_bytes=48 * 1024 * 1024
+            collective_id=0, has_side_effects=True, vmem_limit_bytes=67043328
         ),
-    )(volume, directions, light_dir, tf_center, tf_width, tf_height, tf_emission)
+    )(volume, *parameters)
 
 
 def body(volume, *parameters):

time: 62.6 us -> 54.3 us (0.87)
  local copies, waits for them, and re-layouts: 6.42 us -> 1.57 us
  Pallas kernels: 55.9 us -> 52.4 us
    unnamed x14 -> x1, local copies, waits for them, and re-layouts: 6.42 us -> 1.57 us
    pallas_call x1, Pallas kernels: 55.9 us -> 52.4 us  [fused_body(): pl.pallas_call(functools.partial(kernel, slab * devices, chunks, groups),...]
where the time goes in v1:
time: 54.3 us; the launch traced here: 54 us
  Pallas kernels  52.4 us (97%)
  local copies, waits for them, and re-layouts  1.57 us (3%)
    pallas_call x1, Pallas kernels, fused_body(): pl.pallas_call(functools.partial(kernel, slab * devices, chunks, groups),...  52.4 us
    unnamed x1, local copies, waits for them, and re-layouts  1.57 us

profile of v1, /device:TPU:27, one launch (start us, length us, event | category | flops | bytes accessed | tf_op | source)
XLA Modules:
  0.0 54.0 jit_solution(18382909181682418643)
XLA Ops:
  0.0 52.4 %shard_map.73 = f32[2,4,4096]{2,1,0:T(4,128)} custom-call(bf16[8,128,1024]{2,1,0:T(8,128)(2,1)} %vol.1, s32[2,128]{1,0:T(2,128)} %dirs_in.1, f32[2,3]{1,0:T(2,128)} %light_in.1, f32[2,4]{1,0:T(2,128)} %center_in.1, f32[2,4]{1,0:T(2,128)} %width_in.1, f32[2,4]{1,0:T(2,128)} %height_in.1, f32[3,2,4]{2,1,0:T(2,128)} %bitcast.1), custom_call_target="tpu_custom_call" | custom-call | tf_op jit(solution)/shard_map/pallas_call | solution.py:532
  52.4 1.6 %copy.9 = f32[2,4,4096]{2,1,0:T(4,128)} copy(f32[2,4,4096]{2,1,0:T(4,128)} %shard_map.73) | data formatting | bytes 262144

commit v2 on v1

--- a/solution.py
+++ b/solution.py
@@ -166,7 +166,7 @@
 LOG2E = math.log2(math.e)
 LANES = 256
 ROWS = 16
-LAG_CORE, LAG_Y, LAG_Z0, LAG_Z1, LAG_X = 3, 8, 13, 18, 22
+LAG_CORE, LAG_Y, LAG_Z0, LAG_Z1, LAG_X = 2, 7, 12, 17, 21
 
 
 def kernel(

time: 54.3 us -> 53.9 us (level)
  no operation moved by 1% of the time
where the time goes in v2:
time: 53.9 us; the launch traced here: 53.5 us
  Pallas kernels  51.9 us (96%)
  local copies, waits for them, and re-layouts  1.57 us (3%)
    pallas_call x1, Pallas kernels, fused_body(): pl.pallas_call(functools.partial(kernel, slab * devices, chunks, groups),...  51.9 us
    unnamed x1, local copies, waits for them, and re-layouts  1.57 us

profile of v2, /device:TPU:27, one launch (start us, length us, event | category | flops | bytes accessed | tf_op | source)
XLA Modules:
  0.0 53.5 jit_solution(14217924583617535400)
XLA Ops:
  0.0 51.9 %shard_map.73 = f32[2,4,4096]{2,1,0:T(4,128)} custom-call(bf16[8,128,1024]{2,1,0:T(8,128)(2,1)} %vol.1, s32[2,128]{1,0:T(2,128)} %dirs_in.1, f32[2,3]{1,0:T(2,128)} %light_in.1, f32[2,4]{1,0:T(2,128)} %center_in.1, f32[2,4]{1,0:T(2,128)} %width_in.1, f32[2,4]{1,0:T(2,128)} %height_in.1, f32[3,2,4]{2,1,0:T(2,128)} %bitcast.1), custom_call_target="tpu_custom_call" | custom-call | tf_op jit(solution)/shard_map/pallas_call | solution.py:532
  51.9 1.6 %copy.9 = f32[2,4,4096]{2,1,0:T(4,128)} copy(f32[2,4,4096]{2,1,0:T(4,128)} %shard_map.73) | data formatting | bytes 262144
